TPU v7x, 512 devices: a whole 4x8x8 slice. The times are simulated.
512 devices in a mesh: dp: 8 (over z), frame: 32 (over y_hi, x, core), tile: 2 (over y_lo).
Axes of the slice: x: 4, y: 8 (y_hi: 4, y_lo: 2; y = y_hi * 2 + y_lo), z: 8, core: 2. Of those that a mesh axis runs over, the one named last changes fastest.
Arguments:
- clip_input: bfloat16 [8, 32, 18, 32, 640], P('dp', 'frame', 'tile'), may hold values from -36 to 36
- cotangent: bfloat16 [8, 32, 18, 32, 640], P('dp', 'frame', 'tile'), may hold values from -6 to 6
- norm_gain: float32 [640], replicated, may hold values from 0.25 to 1.75
- conv_weight: bfloat16 [9, 640, 640], P(None, ('frame', 'tile')), may hold values from -0.078125 to 0.078125
- attn_weight: bfloat16 [640, 2560], P(('frame', 'tile')), may hold values from -0.25 to 0.25
- query_gain: float32 [64], replicated, may hold values from 0.5 to 1.5
- key_gain: float32 [64], replicated, may hold values from 0.5 to 1.5
- logit_scale: float32 [10], replicated, may hold values from 0.5 to 4
Outputs:
- mid_grad: bfloat16 [8, 32, 18, 32, 640], P('dp', 'frame', 'tile')
- value_grad: float32 [640, 640], P(('frame', 'tile'))
- out_proj_grad: float32 [640, 640], P(('frame', 'tile'))
- query_gain_grad: float32 [64], replicated
- key_gain_grad: float32 [64], replicated
- scale_grad: float32 [10], replicated
All inputs are finite; a program needn't handle non-finite values.
Results may differ from a plain program's by a relative error of at most 0.013.
The roundings to bfloat16 on the way count: a program that leaves them out, or rounds other values in their place, can miss the bound.
Values may be sent and summed in bfloat16 or wider, within the bound.
A program may use at most 128 MiB of HBM per device.

v0:
```python
import math
import jax
import jax.numpy as jnp
from jax import lax
from jax.sharding import PartitionSpec as P

GROUPS = 32


def extended(x, sides, width):
    for axis, dim in sides:
        devices, length = (lax.axis_size(axis), x.shape[dim])
        up = [(i, (i + 1) % devices) for i in range(devices - 1)]
        down = [(j, i) for i, j in up]
        last = lax.slice_in_dim(x, length - width, length, axis=dim)
        first = lax.slice_in_dim(x, 0, width, axis=dim)
        before = lax.ppermute(last, axis, up)
        after = lax.ppermute(first, axis, down)
        x = jnp.concatenate([before, x, after], axis=dim)
    return x


def layer_stats(vec):
    mean = jnp.mean(vec, axis=-1, keepdims=True)
    cent = vec - mean
    var = jnp.mean(cent * cent, axis=-1, keepdims=True)
    rstd = lax.rsqrt(var + 1e-05)
    return (cent * rstd, rstd)


def layer_back(dhat, hat, rstd):
    first = jnp.mean(dhat, axis=-1, keepdims=True)
    second = jnp.mean(dhat * hat, axis=-1, keepdims=True)
    return rstd * (dhat - first - hat * second)


def attention_pass(mid, cot, weights, query_gain, key_gain, logit_scale):
    frames, count, width = mid.shape
    heads = logit_scale.shape[0]
    depth = width // heads
    total = frames * count
    high = lax.Precision.HIGHEST
    f32 = jnp.float32
    flat = mid.reshape(total, width)
    w_inner = weights[:, : 3 * width]
    proj = jnp.dot(flat, w_inner, preferred_element_type=f32)
    query = proj[:, :width].reshape(frames, count, heads, depth)
    keyed = proj[:, width : 2 * width].reshape(frames, count, heads, depth)
    value = proj[:, 2 * width :].astype(jnp.bfloat16).reshape(frames, count, heads, depth)
    q_hat, q_rstd = layer_stats(query)
    k_hat, k_rstd = layer_stats(keyed)
    q_norm = q_hat * query_gain
    k_norm = k_hat * key_gain
    root = math.sqrt(depth)
    raw = jnp.einsum("fnhd,gnhd->nhfg", q_norm, k_norm, precision=high) / root
    scale = logit_scale[None, :, None, None]
    expo = jnp.exp(raw * scale)
    probs = expo / jnp.sum(expo, axis=-1, keepdims=True)
    probs_b = probs.astype(jnp.bfloat16)
    mixed = jnp.einsum("nhfg,gnhd->fnhd", probs_b, value, preferred_element_type=f32)
    mixed = mixed.astype(jnp.bfloat16).reshape(total, width)
    cot_flat = cot.reshape(total, width)
    w_out = weights[:, 3 * width :]
    d_mixed = lax.dot_general(cot_flat, w_out, (((1,), (1,)), ((), ())), preferred_element_type=f32)
    d_mixed = d_mixed.astype(jnp.bfloat16).reshape(frames, count, heads, depth)
    d_probs = jnp.einsum("fnhd,gnhd->nhfg", d_mixed, value, preferred_element_type=f32)
    d_value = jnp.einsum("nhfg,fnhd->gnhd", probs_b, d_mixed, preferred_element_type=f32)
    d_value = d_value.astype(jnp.bfloat16)
    d_logits = probs * (d_probs - jnp.sum(probs * d_probs, axis=-1, keepdims=True))
    scale_term = jnp.sum(d_logits * raw, axis=(0, 2, 3))
    d_raw = d_logits * scale / root
    d_qn = jnp.einsum("nhfg,gnhd->fnhd", d_raw, k_norm, precision=high)
    d_kn = jnp.einsum("nhfg,fnhd->gnhd", d_raw, q_norm, precision=high)
    qgain_term = jnp.sum(d_qn * q_hat, axis=(0, 1, 2))
    kgain_term = jnp.sum(d_kn * k_hat, axis=(0, 1, 2))
    d_query = layer_back(d_qn * query_gain, q_hat, q_rstd).astype(jnp.bfloat16)
    d_key = layer_back(d_kn * key_gain, k_hat, k_rstd).astype(jnp.bfloat16)
    d_cat = jnp.concatenate(
        [d_query.reshape(total, width), d_key.reshape(total, width), d_value.reshape(total, width)],
        axis=1,
    )
    d_mid = lax.dot_general(d_cat, w_inner, (((1,), (1,)), ((), ())), preferred_element_type=f32)
    d_mid = d_mid.astype(jnp.bfloat16).reshape(frames, count, width)
    return (d_mid, mixed, d_value.reshape(total, width), scale_term, qgain_term, kgain_term)


def local(
    clip_input, cotangent, norm_gain, conv_weight, attn_weight, query_gain, key_gain, logit_scale
):
    source = clip_input[0]
    cot = cotangent[0]
    frames_here, rows, cols, width = source.shape
    positions = rows * cols
    per_group = width // GROUPS
    cot_flat = cot.reshape(frames_here, positions, width)
    attn_full = lax.all_gather(attn_weight, ("frame", "tile"), axis=0, tiled=True)
    xf = source.astype(jnp.float32).reshape(frames_here, positions, GROUPS, per_group)
    sums, squares = lax.psum((jnp.sum(xf, axis=(1, 3)), jnp.sum(xf * xf, axis=(1, 3))), "tile")
    count = positions * lax.axis_size("tile") * per_group
    mean = sums / count
    rstd = lax.rsqrt(squares / count - mean * mean + 1e-05)
    normed = (xf - mean[:, None, :, None]) * rstd[:, None, :, None]
    zed = normed.reshape(frames_here, rows, cols, width) * norm_gain
    act = jax.nn.silu(zed).astype(jnp.bfloat16)
    padded = extended(act, (("tile", 1),), 1)
    padded = jnp.pad(padded, ((0, 0), (0, 0), (1, 1), (0, 0)))
    slabs = []
    for row_off in (-1, 0, 1):
        for col_off in (-1, 0, 1):
            slabs.append(
                padded[:, 1 + row_off : 1 + row_off + rows, 1 + col_off : 1 + col_off + cols, :]
            )
    stacked = jnp.stack(slabs, axis=3).reshape(frames_here * positions, 9, width)
    full_conv = lax.all_gather(conv_weight, ("frame", "tile"), axis=1, tiled=True)
    pre = jnp.dot(
        stacked.reshape(frames_here * positions, 9 * width),
        full_conv.reshape(9 * width, width),
        preferred_element_type=jnp.float32,
    )
    mid = (source.astype(jnp.float32) + pre.reshape(frames_here, rows, cols, width)).astype(
        jnp.bfloat16
    )
    mid_flat = mid.reshape(frames_here, positions, width)
    mid_tiled, cot_tiled = (
        lax.all_to_all(mid_flat, "frame", split_axis=1, concat_axis=0, tiled=True),
        lax.all_to_all(cot_flat, "frame", split_axis=1, concat_axis=0, tiled=True),
    )
    d_mid, mixed, d_value, scale_term, qgain_term, kgain_term = attention_pass(
        mid_tiled, cot_tiled, attn_full, query_gain, key_gain, logit_scale
    )
    d_back = lax.all_to_all(d_mid, "frame", split_axis=0, concat_axis=1, tiled=True)
    mid_grad = (
        cot.astype(jnp.float32) + d_back.reshape(frames_here, rows, cols, width).astype(jnp.float32)
    ).astype(jnp.bfloat16)
    tiled_mid = mid_tiled.reshape(-1, width)
    tiled_cot = cot_tiled.reshape(-1, width)
    contract = (((0,), (0,)), ((), ()))
    value_term = lax.dot_general(tiled_mid, d_value, contract, preferred_element_type=jnp.float32)
    out_term = lax.dot_general(mixed, tiled_cot, contract, preferred_element_type=jnp.float32)
    shares = lax.psum_scatter(
        jnp.concatenate([value_term, out_term], axis=1),
        ("frame", "tile"),
        scatter_dimension=0,
        tiled=True,
    )
    summed = lax.psum(shares.astype(jnp.bfloat16), "dp").astype(jnp.float32)
    scale_sum, qgain_sum, kgain_sum = lax.psum(
        (scale_term, qgain_term, kgain_term), ("dp", "frame", "tile")
    )
    tokens_all = lax.axis_size("dp") * mid_tiled.shape[0] * rows * lax.axis_size("tile") * cols
    factor = 1.0 / math.sqrt(tokens_all)
    value_grad = summed[:, :width] * factor
    out_proj_grad = summed[:, width:] * factor
    return (
        mid_grad[None],
        value_grad,
        out_proj_grad,
        qgain_sum * factor,
        kgain_sum * factor,
        scale_sum * factor,
    )


def solution(mesh):
    in_specs = (
        P("dp", "frame", "tile", None, None),
        P("dp", "frame", "tile", None, None),
        P(),
        P(None, ("frame", "tile"), None),
        P(("frame", "tile"), None),
        P(),
        P(),
        P(),
    )
    out_specs = (
        P("dp", "frame", "tile", None, None),
        P(("frame", "tile"), None),
        P(("frame", "tile"), None),
        P(),
        P(),
        P(),
    )
    return jax.shard_map(local, mesh=mesh, in_specs=in_specs, out_specs=out_specs, check_vma=False)
```

profile of v0, /device:TPU:1, one launch (start us, length us, event | category | flops | bytes accessed | tf_op | source)
XLA Modules:
  0.0 950.0 jit_solution(8612890330028750961)
XLA Ops:
  11.2 4.4 all-reduce.3
  17.0 3.4 collective-permute-start
  22.8 2.9 reduce.8
  26.9 11.3 %all-to-all-start.1 = ((bf16[32,2,2880]{2,1,0:T(2,128)(2,1)}), bf16[32,2,2880]{2,1,0:T(2,128)(2,1)S(1)}, u32[]{:S(2)}, u32[]{:S(2)}) async-start(bf16[32,2,2880]{2,1,0:T(2,128)(2,1)} %reshape.273), calls=%async_computation.1 | async-start | bytes 753664 | tf_op jit(solution)/shard_map/all_to_all | solution.py:126
  39.7 4.1 copy.126
  43.9 7.3 dot_general.38
  51.2 167.2 %all-gather.4.cloned.1.call-done = bf16[9,640,640]{2,0,1:T(8,128)(2,1)} async-done(((bf16[9,10,640]{2,0,1:T(8,128)(2,1)}), bf16[9,640,640]{2,0,1:T(8,128)(2,1)}) %all-gather.4.cloned.1.call-update) | async-done | bytes 7372816 | tf_op jit(solution)/shard_map/all_gather | solution.py:114
  218.4 9.3 copy.128
  227.7 6.9 fusion.26
  235.2 2.9 reduce.9
  239.2 16.7 %all-to-all-start = ((bf16[32,2,2880]{2,1,0:T(2,128)(2,1)}), bf16[32,2,2880]{2,1,0:T(2,128)(2,1)}, u32[]{:S(2)}, u32[]{:S(2)}) async-start(bf16[32,2,2880]{2,1,0:T(2,128)(2,1)} %reshape.275), calls=%async_computation | async-start | bytes 753664 | tf_op jit(solution)/shard_map/all_to_all | solution.py:125
  259.2 164.3 %all-gather.6.cloned.1.call-done = bf16[64,10,2560]{2,1,0:T(8,128)(2,1)} async-done(((bf16[1,10,2560]{2,1,0:T(8,128)(2,1)}), bf16[64,10,2560]{2,1,0:T(8,128)(2,1)}) %all-gather.6.cloned.1.call-update) | async-done | bytes 3276816 | tf_op jit(solution)/shard_map/all_gather | solution.py:96
  423.4 5.3 reshape.268
  428.7 2.9 convolution_convert_fusion.2
  431.6 2.5 reshape.256
  434.2 3.6 reshape.276
  437.7 2.2 fusion.3
  447.5 5.0 multiply_reduce_fusion.4
  453.3 3.0 fusion.18
  458.4 3.0 multiply_reduce_fusion
  461.4 4.5 fusion.5
  465.9 5.9 fusion.6
  473.2 2.7 reshape.262
  475.9 2.5 copy.141
  480.3 2.1 fusion.90
  485.0 284.3 %all-reduce.5 = bf16[640,1280]{0,1:T(8,128)(2,1)} all-reduce(f32[640,1280]{0,1:T(8,128)} %pad_maximum_fusion), channel_id=2, replica_groups=mesh['dp'=8,'frame'=32,'tile'=2] {'frame','tile'}, use_global_device_ids=true, to_apply=%region_16.17.clone | all-reduce | flops 819200 | bytes 4915200
  770.5 28.1 %psum.44 = bf16[10,1280]{0,1:T(8,128)(2,1)} all-reduce(bf16[10,1280]{0,1:T(8,128)(2,1)S(1)} %dynamic-slice_convert_fusion), channel_id=1, replica_groups=mesh['dp'=8,'frame'=32,'tile'=2] {'dp'}, use_global_device_ids=true, to_apply=%region_17.18 | all-reduce | flops 12800 | bytes 51200 | tf_op jit(solution)/shard_map/psum | solution.py:146
  806.2 2.5 reshape.258
  811.5 2.6 reshape.259
  814.1 3.1 fusion.23
  819.2 18.8 %all-to-all-start.2 = ((bf16[32,9,640]{2,1,0:T(8,128)(2,1)}), bf16[32,9,640]{2,1,0:T(8,128)(2,1)S(1)}, u32[]{:S(2)}, u32[]{:S(2)}) async-start(bf16[32,9,640]{2,1,0:T(8,128)(2,1)} %reshape.261), calls=%async_computation.2 | async-start | bytes 1310720 | tf_op jit(solution)/shard_map/all_to_all | solution.py:131
  839.6 100.9 %all-reduce.2 = (f32[64]{0:T(128)S(1)}, f32[64]{0:T(128)S(1)}, f32[10]{0:T(128)S(1)}) all-reduce(f32[64]{0:T(128)S(1)} %get-tuple-element.44, f32[64]{0:T(128)S(1)} %get-tuple-element.42, f32[10]{0:T(128)S(1)} %copy-done.18), channel_id=1, replica_groups=mesh['dp'=8,'frame'=32,'tile'=2] {'dp','frame','tile'}, use_global_device_ids=true, to_apply=%region_19.20 | all-reduce | flops 138 | bytes 1104 | tf_op jit(solution)/shard_map/psum | solution.py:147
  (118 shorter events, 48.4 us)
Async XLA Ops:
  7.2 8.9 copy-start.7
  7.2 14.5 %copy-start.12 = (bf16[1,1,9,32,640]{4,3,2,1,0:T(8,128)(2,1)S(1)}, bf16[1,1,9,32,640]{4,3,2,1,0:T(8,128)(2,1)}, u32[]{:S(2)}) copy-start(bf16[1,1,9,32,640]{4,3,2,1,0:T(8,128)(2,1)} %param.9) | copy-start | bytes 1105924
  7.2 211.2 %all-gather.4.cloned.1.call-start = ((), (), s32[]{:S(2)}) async-start(), calls=%async_computation.3 | async-start | bytes 13312000 | tf_op jit(solution)/shard_map/all_gather | solution.py:114
  9.0 414.5 %all-gather.6.cloned.1.call-start = ((), (), s32[]{:S(2)}) async-start(), calls=%async_computation.4 | async-start | bytes 5324800 | tf_op jit(solution)/shard_map/all_gather | solution.py:96
  17.0 21.2 %collective-permute-start = (bf16[1,1,32,640]{3,2,1,0:T(8,128)(2,1)S(1)}, bf16[1,1,32,640]{3,2,1,0:T(8,128)(2,1)S(1)}, u32[]{:S(2)}, u32[]{:S(2)}) collective-permute-start(bf16[1,1,32,640]{3,2,1,0:T(8,128)(2,1)S(1)} %get-tuple-element.63), channel_id=1, source_target_pairs={{0,1},{2,3},{4,5},{6,7},{8,9},{10,11},{12,13},{14,15},{16,17},{18,... | collective-permute-start | bytes 122888 | tf_op jit(solution)/shard_map/ppermute | solution.py:17
  20.4 17.8 %collective-permute-start.1 = (bf16[1,1,32,640]{3,2,1,0:T(8,128)(2,1)S(1)}, bf16[1,1,32,640]{3,2,1,0:T(8,128)(2,1)S(1)}, u32[]{:S(2)}, u32[]{:S(2)}) collective-permute-start(bf16[1,1,32,640]{3,2,1,0:T(8,128)(2,1)S(1)} %get-tuple-element.64), channel_id=1, source_target_pairs={{1,0},{3,2},{5,4},{7,6},{9,8},{11,10},{13,12},{15,14},{17,16},{19,... | collective-permute-start | bytes 122888 | tf_op jit(solution)/shard_map/ppermute | solution.py:18
  26.9 212.4 %all-to-all-start.1 = ((bf16[32,2,2880]{2,1,0:T(2,128)(2,1)}), bf16[32,2,2880]{2,1,0:T(2,128)(2,1)S(1)}, u32[]{:S(2)}, u32[]{:S(2)}) async-start(bf16[32,2,2880]{2,1,0:T(2,128)(2,1)} %reshape.273), calls=%async_computation.1 | async-start | bytes 753664 | tf_op jit(solution)/shard_map/all_to_all | solution.py:126
  38.4 0.7 copy-start.14
  235.1 22.7 %copy-start.17 = (f32[10]{0:T(128)S(1)}, f32[10]{0:T(128)}, u32[]{:S(2)}) copy-start(f32[10]{0:T(128)} %param.15) | copy-start | bytes 124
  239.2 194.9 %all-to-all-start = ((bf16[32,2,2880]{2,1,0:T(2,128)(2,1)}), bf16[32,2,2880]{2,1,0:T(2,128)(2,1)}, u32[]{:S(2)}, u32[]{:S(2)}) async-start(bf16[32,2,2880]{2,1,0:T(2,128)(2,1)} %reshape.275), calls=%async_computation | async-start | bytes 753664 | tf_op jit(solution)/shard_map/all_to_all | solution.py:125
  428.7 9.0 copy-start.2
  444.1 1.5 copy-start
  446.1 1.4 copy-start.1
  447.5 5.1 copy-start.8
  447.5 5.1 copy-start.9
  452.7 0.7 copy-start.15
  452.7 0.7 copy-start.16
  480.3 2.8 copy-start.11
  480.3 2.1 copy-start.6
  798.7 4.7 copy-start.5
  804.8 3.9 copy-start.4
  810.1 4.0 copy-start.3
  817.1 20.8 %copy-start.10 = (f32[10,1280]{0,1:T(8,128)S(1)}, f32[10,1280]{0,1:T(8,128)}, u32[]{:S(2)}) copy-start(f32[10,1280]{0,1:T(8,128)} %convert_element_type.150) | copy-start | bytes 153604
  819.2 20.4 %copy-start.18 = (f32[10]{0:T(128)S(1)}, f32[10]{0:T(128)}, u32[]{:S(2)}) copy-start(f32[10]{0:T(128)} %get-tuple-element.71) | copy-start | bytes 124
  819.2 122.8 %all-to-all-start.2 = ((bf16[32,9,640]{2,1,0:T(8,128)(2,1)}), bf16[32,9,640]{2,1,0:T(8,128)(2,1)S(1)}, u32[]{:S(2)}, u32[]{:S(2)}) async-start(bf16[32,9,640]{2,1,0:T(8,128)(2,1)} %reshape.261), calls=%async_computation.2 | async-start | bytes 1310720 | tf_op jit(solution)/shard_map/all_to_all | solution.py:131
  837.9 104.2 %copy-start.13 = (bf16[1,1,9,32,640]{4,3,2,1,0:T(8,128)(2,1)S(1)}, bf16[1,1,9,32,640]{4,3,2,1,0:T(8,128)(2,1)}, u32[]{:S(2)}) copy-start(bf16[1,1,9,32,640]{4,3,2,1,0:T(8,128)(2,1)} %param.9) | copy-start | bytes 1105924
Sparse Core Ops, SparseCore 0:
  10.7 207.6 all-gather.3
  220.5 202.8 all-gather.5
where the time goes:
time: 956 us; the launch traced here: 950 us
  blocking collectives  418 us (44%)
  waiting for transfers between devices  332 us (35%)
  local copies, waits for them, and re-layouts  69.5 us (7%)
  starting transfers between devices  51.6 us (5%)
  matrix products  33.7 us (4%)
  other arithmetic  29.8 us (3%)
  between operations  15.5 us (2%)
    unnamed x1, blocking collectives  284 us
    all_gather x1, waiting for transfers between devices, local(): lax.all_gather(conv_weight, ('frame', 'tile'), axis=1, tiled=True)  167 us
    all_gather x1, waiting for transfers between devices, local(): lax.all_gather(attn_weight, ('frame', 'tile'), axis=0, tiled=True)  164 us
    psum x1, blocking collectives, local(): lax.psum((scale_term, qgain_term, kgain_term), ('dp', 'frame', 'tile'))  101 us
    psum x1, blocking collectives, local(): summed = lax.psum(shares.astype(jnp.bfloat16), 'dp').astype(jnp.float32)  28.1 us
    unnamed x53, local copies, waits for them, and re-layouts  19.7 us
  transfers between devices with their start and end apart: 7, of which 2 were waited for; matrix products, arithmetic and copies ran while one was open for 6% of the time, Pallas kernels for 0%

commit v1 on v0

--- a/solution.py
+++ b/solution.py
@@ -93,7 +93,12 @@
     positions = rows * cols
     per_group = width // GROUPS
     cot_flat = cot.reshape(frames_here, positions, width)
-    attn_full = lax.all_gather(attn_weight, ("frame", "tile"), axis=0, tiled=True)
+    attn_full = jnp.concatenate(
+        lax.all_to_all(
+            jnp.stack([attn_weight] * lax.axis_size(("frame", "tile"))), ("frame", "tile"), 0, 0
+        ),
+        axis=0,
+    )
     xf = source.astype(jnp.float32).reshape(frames_here, positions, GROUPS, per_group)
     sums, squares = lax.psum((jnp.sum(xf, axis=(1, 3)), jnp.sum(xf * xf, axis=(1, 3))), "tile")
     count = positions * lax.axis_size("tile") * per_group

time: 956 us -> 869 us (0.909)
  waiting for transfers between devices: 332 us -> 90.2 us
  blocking collectives: 418 us -> 582 us
  starting transfers between devices: 51.6 us -> 40.4 us
    all_gather x1 -> x0, waiting for transfers between devices: 164 us -> none  [local(): lax.all_gather(attn_weight, ('frame', 'tile'), axis=0, tiled=True)]
    psum x1, blocking collectives: 4.43 us -> 137 us  [local(): lax.psum((jnp.sum(xf, axis=(1, 3)), jnp.sum(xf * xf, axis=(1, 3))), 'tile')]
    all_gather x1, waiting for transfers between devices: 167 us -> 85.4 us  [local(): lax.all_gather(conv_weight, ('frame', 'tile'), axis=1, tiled=True)]
    all_to_all x0 -> x1, blocking collectives: none -> 26.4 us  [local(): lax.all_to_all(cot_flat, 'frame', split_axis=1, concat_axis=0, tiled=True)]
    unnamed x53 -> x52, local copies, waits for them, and re-layouts: 19.7 us -> 13.2 us
  transfers between devices with their start and end apart: 7 -> 6, of which waited for: 2 -> 3; matrix products, arithmetic and copies ran while one was open for 6% -> 7% of each run, Pallas kernels for 0% -> 0%
where the time goes in v1:
time: 869 us; the launch traced here: 863 us
  blocking collectives  582 us (67%)
  waiting for transfers between devices  90.2 us (10%)
  local copies, waits for them, and re-layouts  72.3 us (8%)
  starting transfers between devices  40.4 us (5%)
  matrix products  33.7 us (4%)
  other arithmetic  28.4 us (3%)
  between operations  15.4 us (2%)
    unnamed x1, blocking collectives  283 us
    psum x1, blocking collectives, local(): lax.psum((jnp.sum(xf, axis=(1, 3)), jnp.sum(xf * xf, axis=(1, 3))), 'tile')  137 us
    psum x1, blocking collectives, local(): lax.psum((scale_term, qgain_term, kgain_term), ('dp', 'frame', 'tile'))  103 us
    all_gather x1, waiting for transfers between devices, local(): lax.all_gather(conv_weight, ('frame', 'tile'), axis=1, tiled=True)  85.4 us
    psum x1, blocking collectives, local(): summed = lax.psum(shares.astype(jnp.bfloat16), 'dp').astype(jnp.float32)  33.1 us
    all_to_all x1, blocking collectives, local(): lax.all_to_all(cot_flat, 'frame', split_axis=1, concat_axis=0, tiled=True)  26.4 us
    all_to_all x1, starting transfers between devices, local(): lax.all_to_all(mid_flat, 'frame', split_axis=1, concat_axis=0, tiled=True)  18.5 us
  transfers between devices with their start and end apart: 6, of which 3 were waited for; matrix products, arithmetic and copies ran while one was open for 7% of the time, Pallas kernels for 0%

profile of v1, /device:TPU:1, one launch (start us, length us, event | category | flops | bytes accessed | tf_op | source)
XLA Modules:
  0.0 862.7 jit_solution(3128331483565893203)
XLA Ops:
  11.0 2.9 reduce.8
  14.3 26.4 %all_to_all.32 = bf16[32,2,2880]{2,1,0:T(2,128)(2,1)S(1)} all-to-all(bf16[32,2,2880]{2,1,0:T(2,128)(2,1)S(1)} %reshape.277), channel_id=1, replica_groups=mesh['dp'=8,'frame'=32,'tile'=2] {'frame'}, dimensions={0} | all-to-all | bytes 737280 | tf_op jit(solution)/shard_map/all_to_all | solution.py:131
  40.7 3.0 stack.29
  43.7 5.7 all-to-all-start.1
  50.0 136.5 %all-reduce.3 = (f32[1,32]{1,0:T(1,128)S(1)}, f32[1,32]{1,0:T(1,128)S(1)}) all-reduce(f32[1,32]{1,0:T(1,128)S(1)} %bitcast.154, f32[1,32]{1,0:T(1,128)S(1)} %bitcast.153), channel_id=1, replica_groups=mesh['dp'=8,'frame'=32,'tile'=2] {'tile'}, use_global_device_ids=true, to_apply=%region_5.6 | all-reduce | flops 64 | bytes 512 | tf_op jit(solution)/shard_map/psum | solution.py:103
  189.9 4.1 collective-permute-done.1
  195.1 4.1 copy.126
  199.2 7.3 dot_general.38
  206.6 85.4 %all-gather.2.cloned.1.call-done = bf16[9,640,640]{2,0,1:T(8,128)(2,1)} async-done(((bf16[9,10,640]{2,0,1:T(8,128)(2,1)}), bf16[9,640,640]{2,0,1:T(8,128)(2,1)}) %all-gather.2.cloned.1.call-update) | async-done | bytes 7372816 | tf_op jit(solution)/shard_map/all_gather | solution.py:119
  292.0 9.3 %copy.128 = bf16[9,640,640]{2,1,0:T(8,128)(2,1)} copy(bf16[9,640,640]{2,0,1:T(8,128)(2,1)} %all-gather.2.cloned.1.call-done) | data formatting | bytes 14745600 | tf_op jit(solution)/shard_map/all_gather | solution.py:119
  301.3 6.9 fusion.26
  308.8 2.9 reduce.9
  312.8 18.5 %all-to-all-start = ((bf16[32,2,2880]{2,1,0:T(2,128)(2,1)}), bf16[32,2,2880]{2,1,0:T(2,128)(2,1)}, u32[]{:S(2)}, u32[]{:S(2)}) async-start(bf16[32,2,2880]{2,1,0:T(2,128)(2,1)} %reshape.279), calls=%async_computation | async-start | bytes 753664 | tf_op jit(solution)/shard_map/all_to_all | solution.py:130
  334.6 5.3 reshape.258
  339.9 2.9 convolution_convert_fusion.2
  342.8 2.5 reshape.262
  346.0 3.6 reshape.280
  349.6 2.2 fusion.3
  359.4 5.3 multiply_reduce_fusion.4
  365.4 3.0 fusion.18
  370.5 3.0 multiply_reduce_fusion
  373.5 4.5 fusion.5
  378.0 5.9 fusion.6
  385.3 2.7 reshape.268
  388.0 2.5 copy.141
  397.1 283.2 %all-reduce.5 = bf16[640,1280]{0,1:T(8,128)(2,1)} all-reduce(f32[640,1280]{0,1:T(8,128)} %pad_maximum_fusion), channel_id=2, replica_groups=mesh['dp'=8,'frame'=32,'tile'=2] {'frame','tile'}, use_global_device_ids=true, to_apply=%region_16.17.clone | all-reduce | flops 819200 | bytes 4915200
  681.5 33.1 %psum.44 = bf16[10,1280]{0,1:T(8,128)(2,1)} all-reduce(bf16[10,1280]{0,1:T(8,128)(2,1)S(1)} %dynamic-slice_convert_fusion), channel_id=1, replica_groups=mesh['dp'=8,'frame'=32,'tile'=2] {'dp'}, use_global_device_ids=true, to_apply=%region_17.18 | all-reduce | flops 12800 | bytes 51200 | tf_op jit(solution)/shard_map/psum | solution.py:151
  722.1 2.5 reshape.264
  727.4 2.6 reshape.265
  730.0 3.1 fusion.23
  735.1 13.3 %all-to-all-start.3 = ((bf16[32,9,640]{2,1,0:T(8,128)(2,1)}), bf16[32,9,640]{2,1,0:T(8,128)(2,1)S(1)}, u32[]{:S(2)}, u32[]{:S(2)}) async-start(bf16[32,9,640]{2,1,0:T(8,128)(2,1)} %reshape.267), calls=%async_computation.3 | async-start | bytes 1310720 | tf_op jit(solution)/shard_map/all_to_all | solution.py:136
  750.0 103.2 %all-reduce.2 = (f32[64]{0:T(128)S(1)}, f32[64]{0:T(128)S(1)}, f32[10]{0:T(128)S(1)}) all-reduce(f32[64]{0:T(128)S(1)} %get-tuple-element.44, f32[64]{0:T(128)S(1)} %get-tuple-element.42, f32[10]{0:T(128)S(1)} %copy-done.18), channel_id=1, replica_groups=mesh['dp'=8,'frame'=32,'tile'=2] {'dp','frame','tile'}, use_global_device_ids=true, to_apply=%region_19.20 | all-reduce | flops 138 | bytes 1104 | tf_op jit(solution)/shard_map/psum | solution.py:152
  (117 shorter events, 50.0 us)
Async XLA Ops:
  7.2 284.8 %all-gather.2.cloned.1.call-start = ((), (), s32[]{:S(2)}) async-start(), calls=%async_computation.4 | async-start | bytes 13312000 | tf_op jit(solution)/shard_map/all_gather | solution.py:119
  10.4 30.2 %copy-start.13 = (bf16[10,2560]{1,0:T(8,128)(2,1)S(1)}, bf16[10,2560]{1,0:T(8,128)(2,1)}, u32[]{:S(2)}) copy-start(bf16[10,2560]{1,0:T(8,128)(2,1)} %param.12) | copy-start | bytes 153604
  43.7 5.7 copy-start.7
  43.7 143.2 %copy-start.14 = (f32[640]{0:T(1024)S(1)}, f32[640]{0:T(1024)}, u32[]{:S(2)}) copy-start(f32[640]{0:T(1024)} %param.10) | copy-start | bytes 7684
  43.7 269.1 %all-to-all-start.1 = ((bf16[64,10,2560]{2,1,0:T(8,128)(2,1)}), bf16[64,10,2560]{2,1,0:T(8,128)(2,1)}, u32[]{:S(2)}, u32[]{:S(2)}) async-start(bf16[64,10,2560]{2,1,0:T(8,128)(2,1)} %stack.29), calls=%async_computation.1 | async-start | bytes 10485760 | tf_op jit(solution)/shard_map/all_to_all | solution.py:97
  187.2 2.8 collective-permute-start
  188.5 5.6 collective-permute-start.1
  308.7 24.6 %copy-start.17 = (f32[10]{0:T(128)S(1)}, f32[10]{0:T(128)}, u32[]{:S(2)}) copy-start(f32[10]{0:T(128)} %param.15) | copy-start | bytes 124
  312.8 33.2 %all-to-all-start = ((bf16[32,2,2880]{2,1,0:T(2,128)(2,1)}), bf16[32,2,2880]{2,1,0:T(2,128)(2,1)}, u32[]{:S(2)}, u32[]{:S(2)}) async-start(bf16[32,2,2880]{2,1,0:T(2,128)(2,1)} %reshape.279), calls=%async_computation | async-start | bytes 753664 | tf_op jit(solution)/shard_map/all_to_all | solution.py:130
  339.9 9.7 %copy-start.2 = (bf16[640,2560]{1,0:T(8,128)(2,1)}, bf16[640,2560]{1,0:T(8,128)(2,1)S(1)}, u32[]{:S(2)}) copy-start(bf16[640,2560]{1,0:T(8,128)(2,1)S(1)} %reshape.258) | copy-start | bytes 9830404
  356.0 1.5 copy-start
  358.0 1.4 copy-start.1
  359.4 5.4 copy-start.8
  359.4 5.4 copy-start.9
  364.7 0.7 copy-start.15
  364.7 0.7 copy-start.16
  392.4 2.8 copy-start.11
  392.4 2.1 copy-start.6
  714.6 4.7 copy-start.5
  720.7 3.9 copy-start.4
  726.0 4.0 copy-start.3
  733.1 15.3 %copy-start.10 = (f32[10,1280]{0,1:T(8,128)S(1)}, f32[10,1280]{0,1:T(8,128)}, u32[]{:S(2)}) copy-start(f32[10,1280]{0,1:T(8,128)} %convert_element_type.150) | copy-start | bytes 153604
  735.1 14.9 %copy-start.18 = (f32[10]{0:T(128)S(1)}, f32[10]{0:T(128)}, u32[]{:S(2)}) copy-start(f32[10]{0:T(128)} %get-tuple-element.71) | copy-start | bytes 124
  735.1 119.6 %all-to-all-start.3 = ((bf16[32,9,640]{2,1,0:T(8,128)(2,1)}), bf16[32,9,640]{2,1,0:T(8,128)(2,1)S(1)}, u32[]{:S(2)}, u32[]{:S(2)}) async-start(bf16[32,9,640]{2,1,0:T(8,128)(2,1)} %reshape.267), calls=%async_computation.3 | async-start | bytes 1310720 | tf_op jit(solution)/shard_map/all_to_all | solution.py:136
  748.4 106.5 %copy-start.12 = (bf16[1,1,9,32,640]{4,3,2,1,0:T(8,128)(2,1)S(1)}, bf16[1,1,9,32,640]{4,3,2,1,0:T(8,128)(2,1)}, u32[]{:S(2)}) copy-start(bf16[1,1,9,32,640]{4,3,2,1,0:T(8,128)(2,1)} %param.9) | copy-start | bytes 1105924
Sparse Core Ops, SparseCore 0:
  10.7 281.2 all-gather.1
